TPU v7x, 256 devices: a whole 4x4x8 slice. The times are simulated.
256 devices in a mesh: dom: 32 (over y_hi, z, core), hid: 8 (over y_lo, x).
Axes of the slice: x: 4, y: 4 (y_hi: 2, y_lo: 2; y = y_hi * 2 + y_lo), z: 8, core: 2. Of those that a mesh axis runs over, the one named last changes fastest.
Arguments:
- features: bfloat16 [512, 32768], P(None, 'dom'), may hold values from -6 to 6
- weight: bfloat16 [512, 512], P(None, 'hid'), may hold values from -0.25 to 0.25
- band_tiles: bfloat16 [3072, 32768], P(None, 'dom'), may hold values from -0.109375 to 0.109375
- tile_live: int32 [12, 128], P(None, 'dom'), may hold values 0 or 1
- send_rows: int32 [32, 32, 128], P('dom'), may hold values from 0 to 1023
- recv_rows: int32 [32, 32, 128], P('dom'), may hold values from 0 to 1023
- edge_weight: float32 [32, 32, 128], P('dom'), may hold values from 0.25 to 1
- live_slots: int32 [32, 32], P('dom'), may hold values from 96 to 128, as said below
- bias_terms: float32 [512], P('hid'), may hold values from -3 to 3
- cotangent: bfloat16 [512, 32768], P('hid', 'dom'), may hold values from -6 to 6
Outputs:
- output: bfloat16 [512, 32768], P('hid', 'dom')
- feature_grad: bfloat16 [512, 32768], P('hid', 'dom')
- weight_grad: float32 [512, 512], P(None, 'hid')
- bias_grad: float32 [512], P('hid')
Inputs may be any that keep to these rules, and one draw needn't show every extreme that they name: `live_slots`: every reader block has at least one owner block whose list has all 128 slots live.
All inputs are finite; a program needn't handle non-finite values. No bound on the sum of `tile_live` on one device may be relied on, other than what follows from the above.
Results may differ from a plain program's by a relative error of at most 0.0065.
Values may be sent and summed in bfloat16 or wider, within the bound.
A program may use at most 64 MiB of HBM per device.

v0:
```python
import jax
import jax.numpy as jnp
from jax import lax
from jax.sharding import PartitionSpec as P

TILE = 256


def passed_along(block, axis, distance):
    devices = range(lax.axis_size(axis))
    route = [((i - distance) % len(devices), i) for i in devices]
    return lax.ppermute(block, axis, route)


def silu_grad(value):
    gate = jax.nn.sigmoid(value)
    return gate * (1.0 + value * (1.0 - gate))


def on_device(
    features,
    weight,
    band_tiles,
    tile_live,
    send_rows,
    recv_rows,
    edge_weight,
    live_slots,
    bias_terms,
    cotangent,
):
    row_count = features.shape[1]
    local_width = weight.shape[1]
    mapped = lax.dot_general(
        weight, features, (((0,), (0,)), ((), ())), preferred_element_type=jnp.float32
    ).astype(jnp.bfloat16)
    tile_mask = tile_live.astype(jnp.bfloat16)
    dense = (
        band_tiles.reshape(3 * row_count // TILE, TILE, row_count // TILE, TILE)
        * tile_mask[:, None, :, None]
    ).reshape(3 * row_count, row_count)
    summed = jnp.dot(mapped, dense[row_count : 2 * row_count], preferred_element_type=jnp.float32)
    for offset in (0, 2):
        arrived = passed_along(mapped, "dom", 1 - offset)
        summed = summed + jnp.dot(
            arrived,
            dense[offset * row_count : (offset + 1) * row_count],
            preferred_element_type=jnp.float32,
        )
    slot_ids = jnp.arange(send_rows.shape[2])
    slot_weight = edge_weight[0] * (slot_ids[None, :] < live_slots[0][:, None]).astype(jnp.float32)
    outgoing = mapped[:, send_rows[0]]
    incoming = lax.all_to_all(outgoing, "dom", split_axis=1, concat_axis=1, tiled=True)
    weighted = incoming.astype(jnp.float32) * slot_weight[None]
    summed = summed.at[:, recv_rows[0].reshape(-1)].add(weighted.reshape(local_width, -1))
    act = summed + bias_terms[:, None]
    output = jax.nn.silu(act).astype(jnp.bfloat16)
    pre_grad = (cotangent.astype(jnp.float32) * silu_grad(act)).astype(jnp.bfloat16)
    contract = (((1,), (1,)), ((), ()))
    map_grad = lax.dot_general(
        pre_grad, dense[row_count : 2 * row_count], contract, preferred_element_type=jnp.float32
    )
    for offset in (0, 2):
        term = lax.dot_general(
            pre_grad,
            dense[offset * row_count : (offset + 1) * row_count],
            contract,
            preferred_element_type=jnp.float32,
        )
        map_grad = map_grad + passed_along(term, "dom", offset - 1)
    message = (pre_grad.astype(jnp.float32)[:, recv_rows[0]] * slot_weight[None]).astype(
        jnp.bfloat16
    )
    returned = lax.all_to_all(message, "dom", split_axis=1, concat_axis=1, tiled=True)
    map_grad = map_grad.at[:, send_rows[0].reshape(-1)].add(
        returned.astype(jnp.float32).reshape(local_width, -1)
    )
    grad_b = map_grad.astype(jnp.bfloat16)
    weight_part = lax.dot_general(features, grad_b, contract, preferred_element_type=jnp.float32)
    bias_part = jnp.sum(pre_grad.astype(jnp.float32), axis=1)
    weight_grad, bias_grad = lax.psum((weight_part, bias_part), "dom")
    feature_grad = lax.psum_scatter(
        jnp.dot(weight, grad_b, preferred_element_type=jnp.float32),
        "hid",
        scatter_dimension=0,
        tiled=True,
    ).astype(jnp.bfloat16)
    return (output, feature_grad, weight_grad, bias_grad)


def solution(mesh):
    return jax.shard_map(
        on_device,
        mesh=mesh,
        in_specs=(
            P(None, "dom"),
            P(None, "hid"),
            P(None, "dom"),
            P(None, "dom"),
            P("dom", None, None),
            P("dom", None, None),
            P("dom", None, None),
            P("dom", None),
            P("hid"),
            P("hid", "dom"),
        ),
        out_specs=(P("hid", "dom"), P("hid", "dom"), P(None, "hid"), P("hid")),
        check_vma=False,
    )
```

profile of v0, /device:TPU:2, one launch (start us, length us, event | category | flops | bytes accessed | tf_op | source)
XLA Modules:
  0.0 441.8 jit_solution(8998535476931524258)
XLA Ops:
  8.0 1.2 copy-done
  9.2 1.1 convolution_convert_fusion
  10.5 8.0 %collective-permute-start.1 = (bf16[64,1024]{1,0:T(8,128)(2,1)S(1)}, bf16[64,1024]{1,0:T(8,128)(2,1)}, u32[]{:S(2)}, u32[]{:S(2)}) collective-permute-start(bf16[64,1024]{1,0:T(8,128)(2,1)S(1)} %convolution_convert_fusion), channel_id=1, source_target_pairs={{8,0},{16,8},{24,16},{32,24},{40,32},{48,40},{56,48},{64,56},{72,6... | collective-permute-start | bytes 393224 | tf_op jit(solution)/shard_map/ppermute | solution.py:12
  19.4 12.1 %gather_fusion = bf16[4096,64]{1,0:T(8,128)(2,1)S(1)} fusion(bf16[64,1024]{0,1:T(8,128)(2,1)S(1)} %copy.31, s32[4096]{0:T(1024)S(1)} %fusion.6), kind=kCustom, calls=%fused_computation | custom fusion | bytes 1064960 | tf_op jit(solution)/shard_map/gather | solution.py:52
  32.6 6.6 %all-to-all-start = ((bf16[64,32,128]{2,0,1:T(8,128)(2,1)}), bf16[64,32,128]{2,0,1:T(8,128)(2,1)}, u32[]{:S(2)}, u32[]{:S(2)}) async-start(bf16[64,32,128]{2,0,1:T(8,128)(2,1)} %bitcast.5), calls=%async_computation | async-start | bytes 1048576 | tf_op jit(solution)/shard_map/all_to_all | solution.py:53
  39.2 11.2 %reshape.173 = bf16[12,256,4,256]{3,2,1,0:T(4,128)(2,1)} reshape(bf16[3072,1024]{1,0:T(8,128)(2,1)} %param.12) | data formatting | bytes 12582912 | tf_op jit(solution)/shard_map/reshape | solution.py:39
  50.5 8.2 %broadcast_multiply_fusion = bf16[12,256,4,256]{3,2,1,0:T(4,128)(2,1)} fusion(bf16[12,256,4,256]{3,2,1,0:T(4,128)(2,1)} %reshape.173, bf16[12,4]{1,0:T(8,128)(2,1)S(1)} %copy.30), kind=kLoop, calls=%fused_computation.4 | loop fusion | flops 3145728 | bytes 12583008 | tf_op jit(solution)/shard_map/mul | solution.py:39
  58.6 4.1 fusion.9
  64.5 2.0 copy.49
  67.2 1.8 copy.36
  69.9 1.3 fusion.8
  71.2 1.4 convolution_add_fusion.2
  72.6 1.4 fusion.1
  75.4 1.9 copy.35
  77.3 23.1 %scatter_fusion = f32[64,1024]{0,1:T(8,128)S(1)} fusion(f32[64,1024]{0,1:T(8,128)S(1)} %copy.34, s32[4096]{0:T(1024)S(1)} %bitcast.79, f32[4096,64]{1,0:T(8,128)} %copy.35), kind=kCustom, calls=%fused_computation.2 | custom fusion | flops 262144 | bytes 3162112 | tf_op jit(solution)/shard_map/scatter-add | solution.py:55
  101.4 3.1 fusion.11
  104.4 1.5 fusion.12
  106.0 5.2 %collective-permute-start.2 = (f32[64,1024]{1,0:T(8,128)}, f32[64,1024]{1,0:T(8,128)}, u32[]{:S(2)}, u32[]{:S(2)}) collective-permute-start(f32[64,1024]{1,0:T(8,128)} %fusion.11), channel_id=1, source_target_pairs={{8,0},{16,8},{24,16},{32,24},{40,32},{48,40},{56,48},{64,56},{72,6... | collective-permute-start | bytes 786440 | tf_op jit(solution)/shard_map/ppermute | solution.py:12
  111.2 14.2 %gather_fusion.1 = f32[4096,64]{1,0:T(8,128)} fusion(f32[64,1024]{0,1:T(8,128)S(1)} %convert_element_type.39, s32[4096]{0:T(1024)S(1)} %copy-done.9), kind=kCustom, calls=%fused_computation.1 | custom fusion | bytes 2113536 | tf_op jit(solution)/shard_map/gather | solution.py:71
  125.4 3.1 copy.37
  128.5 2.3 fusion.2
  130.8 7.1 %all-to-all-start.1 = ((bf16[64,32,128]{2,0,1:T(8,128)(2,1)}), bf16[64,32,128]{2,0,1:T(8,128)(2,1)}, u32[]{:S(2)}, u32[]{:S(2)}) async-start(bf16[64,32,128]{2,0,1:T(8,128)(2,1)} %fusion.2), calls=%async_computation.1 | async-start | bytes 1048576 | tf_op jit(solution)/shard_map/all_to_all | solution.py:74
  138.1 2.5 fusion
  140.6 1.1 copy.39
  141.8 16.1 %all-to-all-done.1 = bf16[64,32,128]{2,0,1:T(8,128)(2,1)} async-done(((bf16[64,32,128]{2,0,1:T(8,128)(2,1)}), bf16[64,32,128]{2,0,1:T(8,128)(2,1)}, u32[]{:S(2)}, u32[]{:S(2)}) %all-to-all-start.1) | async-done | bytes 524320 | tf_op jit(solution)/shard_map/all_to_all | solution.py:74
  159.0 1.9 copy.40
  160.9 22.9 %scatter_fusion.1 = f32[64,1024]{0,1:T(8,128)S(1)} fusion(f32[64,1024]{0,1:T(8,128)S(1)} %copy.39, s32[4096]{0:T(1024)S(1)} %bitcast.80, f32[4096,64]{1,0:T(8,128)} %copy.40), kind=kCustom, calls=%fused_computation.3 | custom fusion | flops 262144 | bytes 3162112 | tf_op jit(solution)/shard_map/scatter-add | solution.py:75
  183.8 1.7 convolution_bitcast_fusion
  185.6 2.9 copy.43
  190.5 65.5 %psum.15 = f32[64]{0:T(128)} all-reduce(f32[64]{0:T(128)S(1)} %get-tuple-element.16), channel_id=1, replica_groups=mesh['dom'=32,'hid'=8] {'dom'}, use_global_device_ids=true, to_apply=%region_5.6 | all-reduce | flops 64 | bytes 512 | tf_op jit(solution)/shard_map/psum | solution.py:81
  257.9 174.9 %all-reduce.2.cloned.1.call-done = f32[512,64]{0,1:T(8,128)} async-done(((f32[512,64]{0,1:T(8,128)}), f32[512,64]{0,1:T(8,128)}) %all-reduce.2.cloned.1.call-update) | async-done | bytes 131088 | tf_op jit(solution)/shard_map/psum | solution.py:81
  432.8 1.6 copy.55
  (59 shorter events, 13.0 us)
Async XLA Ops:
  8.0 1.2 copy-start
  10.4 60.8 %collective-permute-start = (bf16[64,1024]{1,0:T(8,128)(2,1)S(1)}, bf16[64,1024]{1,0:T(8,128)(2,1)}, u32[]{:S(2)}, u32[]{:S(2)}) collective-permute-start(bf16[64,1024]{1,0:T(8,128)(2,1)S(1)} %convolution_convert_fusion), channel_id=1, source_target_pairs={{248,0},{0,8},{8,16},{16,24},{24,32},{32,40},{40,48},{48,56},{56,6... | collective-permute-start | bytes 393224 | tf_op jit(solution)/shard_map/ppermute | solution.py:12
  10.5 62.2 %collective-permute-start.1 = (bf16[64,1024]{1,0:T(8,128)(2,1)S(1)}, bf16[64,1024]{1,0:T(8,128)(2,1)}, u32[]{:S(2)}, u32[]{:S(2)}) collective-permute-start(bf16[64,1024]{1,0:T(8,128)(2,1)S(1)} %convolution_convert_fusion), channel_id=1, source_target_pairs={{8,0},{16,8},{24,16},{32,24},{40,32},{48,40},{56,48},{64,56},{72,6... | collective-permute-start | bytes 393224 | tf_op jit(solution)/shard_map/ppermute | solution.py:12
  32.6 41.6 %all-to-all-start = ((bf16[64,32,128]{2,0,1:T(8,128)(2,1)}), bf16[64,32,128]{2,0,1:T(8,128)(2,1)}, u32[]{:S(2)}, u32[]{:S(2)}) async-start(bf16[64,32,128]{2,0,1:T(8,128)(2,1)} %bitcast.5), calls=%async_computation | async-start | bytes 1048576 | tf_op jit(solution)/shard_map/all_to_all | solution.py:53
  39.2 11.2 %copy-start.13 = (s32[12,4]{0,1:T(4,128)S(1)}, s32[12,4]{0,1:T(4,128)}, u32[]{:S(2)}) copy-start(s32[12,4]{0,1:T(4,128)} %param.13) | copy-start | bytes 580
  63.2 1.3 copy-start.4
  64.5 6.7 %copy-start.1 = (bf16[128,8,4,256]{3,1,2,0:T(8,128)(2,1)}, bf16[128,8,4,256]{3,1,2,0:T(8,128)(2,1)S(1)}, u32[]{:S(2)}) copy-start(bf16[128,8,4,256]{3,1,2,0:T(8,128)(2,1)S(1)} %copy.48) | copy-start | bytes 6291460
  64.5 2.0 copy-start.11
  68.9 3.7 copy-start.2
  74.2 3.1 copy-start.10
  77.3 23.1 %copy-start.7 = (bf16[64,1024]{0,1:T(8,128)(2,1)S(1)}, bf16[64,1024]{0,1:T(8,128)(2,1)}, u32[]{:S(2)}) copy-start(bf16[64,1024]{0,1:T(8,128)(2,1)} %copy.36) | copy-start | bytes 393220
  100.4 4.1 copy-start.3
  104.4 6.8 %copy-start.9 = (s32[4096]{0:T(1024)S(1)}, s32[4096]{0:T(1024)}, u32[]{:S(2)}) copy-start(s32[4096]{0:T(1024)} %fusion.8) | copy-start | bytes 49156
  106.0 32.1 %collective-permute-start.2 = (f32[64,1024]{1,0:T(8,128)}, f32[64,1024]{1,0:T(8,128)}, u32[]{:S(2)}, u32[]{:S(2)}) collective-permute-start(f32[64,1024]{1,0:T(8,128)} %fusion.11), channel_id=1, source_target_pairs={{8,0},{16,8},{24,16},{32,24},{40,32},{48,40},{56,48},{64,56},{72,6... | collective-permute-start | bytes 786440 | tf_op jit(solution)/shard_map/ppermute | solution.py:12
  111.2 26.9 %collective-permute-start.3 = (f32[64,1024]{1,0:T(8,128)}, f32[64,1024]{1,0:T(8,128)}, u32[]{:S(2)}, u32[]{:S(2)}) collective-permute-start(f32[64,1024]{1,0:T(8,128)} %fusion.12), channel_id=1, source_target_pairs={{248,0},{0,8},{8,16},{16,24},{24,32},{32,40},{40,48},{48,56},{56,6... | collective-permute-start | bytes 786440 | tf_op jit(solution)/shard_map/ppermute | solution.py:12
  128.5 9.5 %copy-start.12 = (s32[1,32,128]{2,1,0:T(8,128)S(1)}, s32[1,32,128]{2,1,0:T(8,128)}, u32[]{:S(2)}) copy-start(s32[1,32,128]{2,1,0:T(8,128)} %param.14) | copy-start | bytes 49156
  128.5 9.6 %copy-start.5 = (bf16[128,8,4,256]{3,1,2,0:T(8,128)(2,1)S(1)}, bf16[128,8,4,256]{3,1,2,0:T(8,128)(2,1)}, u32[]{:S(2)}) copy-start(bf16[128,8,4,256]{3,1,2,0:T(8,128)(2,1)} %copy-done.4) | copy-start | bytes 6291460
  130.8 27.1 %all-to-all-start.1 = ((bf16[64,32,128]{2,0,1:T(8,128)(2,1)}), bf16[64,32,128]{2,0,1:T(8,128)(2,1)}, u32[]{:S(2)}, u32[]{:S(2)}) async-start(bf16[64,32,128]{2,0,1:T(8,128)(2,1)} %fusion.2), calls=%async_computation.1 | async-start | bytes 1048576 | tf_op jit(solution)/shard_map/all_to_all | solution.py:74
  138.0 118.0 %reduce-scatter.4.cloned.1.call-start = ((), (), s32[]{:S(2)}) async-start(), calls=%async_computation.4 | async-start | bytes 2359296
  160.9 22.9 %copy-start.8 = (bf16[512,64]{0,1:T(8,128)(2,1)S(1)}, bf16[512,64]{0,1:T(8,128)(2,1)}, u32[]{:S(2)}) copy-start(bf16[512,64]{0,1:T(8,128)(2,1)} %param.11) | copy-start | bytes 196612
  188.5 1.2 copy-start.6
  188.5 244.3 %all-reduce.2.cloned.1.call-start = ((), (), s32[]{:S(2)}) async-start(), calls=%async_computation.3 | async-start | bytes 262144 | tf_op jit(solution)/shard_map/psum | solution.py:81
Sparse Core Ops, SparseCore 0:
  188.6 36.9 reduce-scatter.3
Sparse Core Ops, SparseCore 1:
  192.2 240.6 all-reduce.1
where the time goes:
time: 443 us; the launch traced here: 442 us
  waiting for transfers between devices  191 us (43%)
  blocking collectives  65.5 us (15%)
  local copies, waits for them, and re-layouts  64.8 us (15%)
  other arithmetic  63.3 us (14%)
  starting transfers between devices  27.1 us (6%)
  between operations  15.8 us (4%)
  matrix products  14.3 us (3%)
    psum x1, waiting for transfers between devices, on_device(): weight_grad, bias_grad = lax.psum((weight_part, bias_part), 'dom')  175 us
    psum x1, blocking collectives, on_device(): weight_grad, bias_grad = lax.psum((weight_part, bias_part), 'dom')  65.5 us
    scatter-add x1, other arithmetic, on_device(): summed.at[:, recv_rows[0].reshape(-1)]  23.1 us
    scatter-add x1, other arithmetic, on_device(): map_grad.at[:, send_rows[0].reshape(-1)]  22.9 us
    gather x2, local copies, waits for them, and re-layouts, on_device(): pre_grad.astype(jnp.float32)[:, recv_rows[0]] * slot_weight[None]  17.3 us
    all_to_all x1, waiting for transfers between devices, on_device(): lax.all_to_all(message, 'dom', split_axis=1, concat_axis=1, tiled=True)  16.1 us
    unnamed x37, local copies, waits for them, and re-layouts  13.5 us
    ppermute x4, starting transfers between devices, passed_along(): return lax.ppermute(block, axis, route)  13.3 us
  transfers between devices with their start and end apart: 8, of which 2 were waited for; matrix products, arithmetic and copies ran while one was open for 17% of the time, Pallas kernels for 0%

commit v1 on v0

--- a/solution.py
+++ b/solution.py
@@ -71,7 +71,10 @@
     message = (pre_grad.astype(jnp.float32)[:, recv_rows[0]] * slot_weight[None]).astype(
         jnp.bfloat16
     )
-    returned = lax.all_to_all(message, "dom", split_axis=1, concat_axis=1, tiled=True)
+    returned = jnp.concatenate(
+        lax.all_to_all(jnp.stack(jnp.split(message, lax.axis_size("dom"), axis=1)), "dom", 0, 0),
+        axis=1,
+    )
     map_grad = map_grad.at[:, send_rows[0].reshape(-1)].add(
         returned.astype(jnp.float32).reshape(local_width, -1)
     )

time: 443 us -> 464 us (1.047)
  local copies, waits for them, and re-layouts: 64.8 us -> 85.9 us
    unnamed x37 -> x73, local copies, waits for them, and re-layouts: 13.5 us -> 33.4 us
    all_to_all x1, waiting for transfers between devices: 16.1 us -> 0.01 us  [on_device(): lax.all_to_all(jnp.stack(jnp.split(message, lax.axis_size('dom'), axis=1)...]
    ppermute x4, waiting for transfers between devices: 0.01 us -> 15.2 us  [passed_along(): return lax.ppermute(block, axis, route)]
  transfers between devices with their start and end apart: 8 -> 8, of which waited for: 2 -> 3; matrix products, arithmetic and copies ran while one was open for 17% -> 12% of each run, Pallas kernels for 0% -> 0%
where the time goes in v1:
time: 464 us; the launch traced here: 463 us
  waiting for transfers between devices  192 us (41%)
  local copies, waits for them, and re-layouts  85.9 us (19%)
  blocking collectives  65.5 us (14%)
  other arithmetic  61.7 us (13%)
  starting transfers between devices  29.8 us (6%)
  between operations  15.8 us (3%)
  matrix products  12.5 us (3%)
    psum x1, waiting for transfers between devices, on_device(): weight_grad, bias_grad = lax.psum((weight_part, bias_part), 'dom')  177 us
    psum x1, blocking collectives, on_device(): weight_grad, bias_grad = lax.psum((weight_part, bias_part), 'dom')  65.5 us
    unnamed x73, local copies, waits for them, and re-layouts  33.4 us
    scatter-add x1, other arithmetic, on_device(): summed.at[:, recv_rows[0].reshape(-1)]  23.1 us
    scatter-add x1, other arithmetic, on_device(): map_grad.at[:, send_rows[0].reshape(-1)]  22.9 us
    gather x2, local copies, waits for them, and re-layouts, on_device(): pre_grad.astype(jnp.float32)[:, recv_rows[0]] * slot_weight[None]  17.3 us
    ppermute x4, waiting for transfers between devices, passed_along(): return lax.ppermute(block, axis, route)  15.2 us
    ppermute x4, starting transfers between devices, passed_along(): return lax.ppermute(block, axis, route)  13.3 us
  transfers between devices with their start and end apart: 8, of which 3 were waited for; matrix products, arithmetic and copies ran while one was open for 12% of the time, Pallas kernels for 0%

profile of v1, /device:TPU:2, one launch (start us, length us, event | category | flops | bytes accessed | tf_op | source)
XLA Modules:
  0.0 463.3 jit_solution(15642863931123043049)
XLA Ops:
  8.0 1.2 copy-done
  10.5 8.0 %collective-permute-start.1 = (bf16[64,1024]{1,0:T(8,128)(2,1)S(1)}, bf16[64,1024]{1,0:T(8,128)(2,1)S(1)}, u32[]{:S(2)}, u32[]{:S(2)}) collective-permute-start(bf16[64,1024]{1,0:T(8,128)(2,1)S(1)} %convolution_convert_fusion), channel_id=1, source_target_pairs={{8,0},{16,8},{24,16},{32,24},{40,32},{48,40},{56,48},{64,56},{72,6... | collective-permute-start | bytes 393224 | tf_op jit(solution)/shard_map/ppermute | solution.py:12
  18.6 1.4 fusion.6
  20.0 12.1 %gather_fusion = bf16[4096,64]{1,0:T(8,128)(2,1)S(1)} fusion(bf16[64,1024]{0,1:T(8,128)(2,1)S(1)} %copy.31, s32[4096]{0:T(1024)S(1)} %get-tuple-element.22), kind=kCustom, calls=%fused_computation | custom fusion | bytes 1064960 | tf_op jit(solution)/shard_map/gather | solution.py:52
  33.3 6.6 %all-to-all-start = ((bf16[64,32,128]{2,0,1:T(8,128)(2,1)}), bf16[64,32,128]{2,0,1:T(8,128)(2,1)}, u32[]{:S(2)}, u32[]{:S(2)}) async-start(bf16[64,32,128]{2,0,1:T(8,128)(2,1)} %bitcast.5), calls=%async_computation | async-start | bytes 1048576 | tf_op jit(solution)/shard_map/all_to_all | solution.py:53
  39.8 11.2 %reshape.173 = bf16[12,256,4,256]{3,2,1,0:T(4,128)(2,1)} reshape(bf16[3072,1024]{1,0:T(8,128)(2,1)} %param.12) | data formatting | bytes 12582912 | tf_op jit(solution)/shard_map/reshape | solution.py:39
  51.1 8.2 %broadcast_multiply_fusion = bf16[12,256,4,256]{3,2,1,0:T(4,128)(2,1)} fusion(bf16[12,256,4,256]{3,2,1,0:T(4,128)(2,1)} %reshape.173, bf16[12,4]{1,0:T(8,128)(2,1)S(1)} %copy.30), kind=kLoop, calls=%fused_computation.4 | loop fusion | flops 3145728 | bytes 12583008 | tf_op jit(solution)/shard_map/mul | solution.py:39
  59.3 4.1 fusion.9
  63.3 1.8 copy.46
  65.7 2.0 copy.48
  69.2 2.2 fusion.10
  72.2 1.4 convolution_add_fusion.2
  75.4 1.9 copy.35
  77.4 23.1 %scatter_fusion = f32[64,1024]{0,1:T(8,128)S(1)} fusion(f32[64,1024]{0,1:T(8,128)S(1)} %copy.34, s32[4096]{0:T(1024)S(1)} %bitcast.214, f32[4096,64]{1,0:T(8,128)} %copy.35), kind=kCustom, calls=%fused_computation.2 | custom fusion | flops 262144 | bytes 3162112 | tf_op jit(solution)/shard_map/scatter-add | solution.py:55
  102.1 1.5 fusion.11
  103.6 1.5 fusion.12
  105.1 14.1 %gather_fusion.1 = f32[4096,64]{1,0:T(8,128)} fusion(f32[64,1024]{0,1:T(8,128)S(1)} %convert_element_type.48, s32[4096]{0:T(1024)S(1)} %copy-done.11), kind=kCustom, calls=%fused_computation.1 | custom fusion | bytes 2113536 | tf_op jit(solution)/shard_map/gather | solution.py:71
  119.2 3.1 copy.37
  122.4 1.5 fusion.2
  143.1 9.9 %all-to-all-start.1 = ((bf16[32,64,1,128]{3,1,2,0:T(8,128)(2,1)}), bf16[32,64,1,128]{3,1,2,0:T(8,128)(2,1)}, u32[]{:S(2)}, u32[]{:S(2)}) async-start(bf16[32,64,1,128]{3,1,2,0:T(8,128)(2,1)} %constant_dynamic-update-slice_fusion), calls=%async_computation.1 | async-start | bytes 1048576 | tf_op jit(solution)/shard_map/all_to_all | solution.py:75
  153.0 5.2 %collective-permute-start.2 = (f32[64,1024]{1,0:T(8,128)}, f32[64,1024]{1,0:T(8,128)S(1)}, u32[]{:S(2)}, u32[]{:S(2)}) collective-permute-start(f32[64,1024]{1,0:T(8,128)} %fusion.11), channel_id=1, source_target_pairs={{8,0},{16,8},{24,16},{32,24},{40,32},{48,40},{56,48},{64,56},{72,6... | collective-permute-start | bytes 786440 | tf_op jit(solution)/shard_map/ppermute | solution.py:12
  158.3 9.5 %collective-permute-done.2 = f32[64,1024]{1,0:T(8,128)S(1)} collective-permute-done((f32[64,1024]{1,0:T(8,128)}, f32[64,1024]{1,0:T(8,128)S(1)}, u32[]{:S(2)}, u32[]{:S(2)}) %collective-permute-start.2) | collective-permute-done | bytes 262176 | tf_op jit(solution)/shard_map/ppermute | solution.py:12
  167.8 5.7 %collective-permute-done.3 = f32[64,1024]{1,0:T(8,128)S(1)} collective-permute-done((f32[64,1024]{1,0:T(8,128)}, f32[64,1024]{1,0:T(8,128)S(1)}, u32[]{:S(2)}, u32[]{:S(2)}) %collective-permute-start.3) | collective-permute-done | bytes 262176 | tf_op jit(solution)/shard_map/ppermute | solution.py:12
  173.5 1.5 fusion
  176.1 1.1 convert_bitcast_fusion
  178.5 1.9 copy.40
  180.4 22.9 %scatter_fusion.1 = f32[64,1024]{0,1:T(8,128)S(1)} fusion(f32[64,1024]{0,1:T(8,128)S(1)} %copy.39, s32[4096]{0:T(1024)S(1)} %bitcast.213, f32[4096,64]{1,0:T(8,128)} %copy.40), kind=kCustom, calls=%fused_computation.3 | custom fusion | flops 262144 | bytes 3162112 | tf_op jit(solution)/shard_map/scatter-add | solution.py:78
  203.3 1.7 convolution_bitcast_fusion
  205.1 2.9 copy.43
  210.0 65.5 %psum.15 = f32[64]{0:T(128)} all-reduce(f32[64]{0:T(128)S(1)} %get-tuple-element.16), channel_id=1, replica_groups=mesh['dom'=32,'hid'=8] {'dom'}, use_global_device_ids=true, to_apply=%region_5.6 | all-reduce | flops 64 | bytes 512 | tf_op jit(solution)/shard_map/psum | solution.py:84
  277.4 176.9 %all-reduce.2.cloned.1.call-done = f32[512,64]{0,1:T(8,128)} async-done(((f32[512,64]{0,1:T(8,128)}), f32[512,64]{0,1:T(8,128)}) %all-reduce.2.cloned.1.call-update) | async-done | bytes 131088 | tf_op jit(solution)/shard_map/psum | solution.py:84
  454.3 1.6 copy.87
  (96 shorter events, 34.4 us)
Async XLA Ops:
  8.0 1.2 copy-start
  10.4 61.8 %collective-permute-start = (bf16[64,1024]{1,0:T(8,128)(2,1)S(1)}, bf16[64,1024]{1,0:T(8,128)(2,1)}, u32[]{:S(2)}, u32[]{:S(2)}) collective-permute-start(bf16[64,1024]{1,0:T(8,128)(2,1)S(1)} %convolution_convert_fusion), channel_id=1, source_target_pairs={{248,0},{0,8},{8,16},{16,24},{24,32},{32,40},{40,48},{48,56},{56,6... | collective-permute-start | bytes 393224 | tf_op jit(solution)/shard_map/ppermute | solution.py:12
  10.5 63.1 %collective-permute-start.1 = (bf16[64,1024]{1,0:T(8,128)(2,1)S(1)}, bf16[64,1024]{1,0:T(8,128)(2,1)S(1)}, u32[]{:S(2)}, u32[]{:S(2)}) collective-permute-start(bf16[64,1024]{1,0:T(8,128)(2,1)S(1)} %convolution_convert_fusion), channel_id=1, source_target_pairs={{8,0},{16,8},{24,16},{32,24},{40,32},{48,40},{56,48},{64,56},{72,6... | collective-permute-start | bytes 393224 | tf_op jit(solution)/shard_map/ppermute | solution.py:12
  33.3 41.0 %all-to-all-start = ((bf16[64,32,128]{2,0,1:T(8,128)(2,1)}), bf16[64,32,128]{2,0,1:T(8,128)(2,1)}, u32[]{:S(2)}, u32[]{:S(2)}) async-start(bf16[64,32,128]{2,0,1:T(8,128)(2,1)} %bitcast.5), calls=%async_computation | async-start | bytes 1048576 | tf_op jit(solution)/shard_map/all_to_all | solution.py:53
  39.8 11.2 %copy-start.14 = (s32[12,4]{0,1:T(4,128)S(1)}, s32[12,4]{0,1:T(4,128)}, u32[]{:S(2)}) copy-start(s32[12,4]{0,1:T(4,128)} %param.13) | copy-start | bytes 580
  65.7 6.5 %copy-start.1 = (bf16[128,8,4,256]{3,1,2,0:T(8,128)(2,1)}, bf16[128,8,4,256]{3,1,2,0:T(8,128)(2,1)S(1)}, u32[]{:S(2)}) copy-start(bf16[128,8,4,256]{3,1,2,0:T(8,128)(2,1)S(1)} %copy.47) | copy-start | bytes 6291460
  65.7 2.0 copy-start.12
  65.7 2.6 copy-start.9
  69.1 4.4 copy-start.3
  69.1 4.4 copy-start.15
  74.3 3.1 copy-start.10
  77.4 23.1 %copy-start.7 = (bf16[64,1024]{0,1:T(8,128)(2,1)S(1)}, bf16[64,1024]{0,1:T(8,128)(2,1)}, u32[]{:S(2)}) copy-start(bf16[64,1024]{0,1:T(8,128)(2,1)} %copy.36) | copy-start | bytes 393220
  100.5 1.7 copy-start.2
  100.5 3.2 copy-start.4
  102.1 3.0 copy-start.11
  122.4 35.9 %copy-start.13 = (s32[1,32,128]{2,1,0:T(8,128)S(1)}, s32[1,32,128]{2,1,0:T(8,128)}, u32[]{:S(2)}) copy-start(s32[1,32,128]{2,1,0:T(8,128)} %param.14) | copy-start | bytes 49156
  122.4 51.1 %copy-start.5 = (bf16[128,8,4,256]{3,1,2,0:T(8,128)(2,1)S(1)}, bf16[128,8,4,256]{3,1,2,0:T(8,128)(2,1)}, u32[]{:S(2)}) copy-start(bf16[128,8,4,256]{3,1,2,0:T(8,128)(2,1)} %copy.46) | copy-start | bytes 6291460
  143.1 33.0 %all-to-all-start.1 = ((bf16[32,64,1,128]{3,1,2,0:T(8,128)(2,1)}), bf16[32,64,1,128]{3,1,2,0:T(8,128)(2,1)}, u32[]{:S(2)}, u32[]{:S(2)}) async-start(bf16[32,64,1,128]{3,1,2,0:T(8,128)(2,1)} %constant_dynamic-update-slice_fusion), calls=%async_computation.1 | async-start | bytes 1048576 | tf_op jit(solution)/shard_map/all_to_all | solution.py:75
  153.0 122.5 %reduce-scatter.4.cloned.1.call-start = ((), (), s32[]{:S(2)}) async-start(), calls=%async_computation.4 | async-start | bytes 2359296
  153.0 14.7 %collective-permute-start.2 = (f32[64,1024]{1,0:T(8,128)}, f32[64,1024]{1,0:T(8,128)S(1)}, u32[]{:S(2)}, u32[]{:S(2)}) collective-permute-start(f32[64,1024]{1,0:T(8,128)} %fusion.11), channel_id=1, source_target_pairs={{8,0},{16,8},{24,16},{32,24},{40,32},{48,40},{56,48},{64,56},{72,6... | collective-permute-start | bytes 786440 | tf_op jit(solution)/shard_map/ppermute | solution.py:12
  158.3 15.2 %collective-permute-start.3 = (f32[64,1024]{1,0:T(8,128)}, f32[64,1024]{1,0:T(8,128)S(1)}, u32[]{:S(2)}, u32[]{:S(2)}) collective-permute-start(f32[64,1024]{1,0:T(8,128)} %fusion.12), channel_id=1, source_target_pairs={{248,0},{0,8},{8,16},{16,24},{24,32},{32,40},{40,48},{48,56},{56,6... | collective-permute-start | bytes 786440 | tf_op jit(solution)/shard_map/ppermute | solution.py:12
  180.4 22.9 %copy-start.8 = (bf16[512,64]{0,1:T(8,128)(2,1)S(1)}, bf16[512,64]{0,1:T(8,128)(2,1)}, u32[]{:S(2)}) copy-start(bf16[512,64]{0,1:T(8,128)(2,1)} %param.11) | copy-start | bytes 196612
  208.0 1.2 copy-start.6
  208.0 246.3 %all-reduce.2.cloned.1.call-start = ((), (), s32[]{:S(2)}) async-start(), calls=%async_computation.3 | async-start | bytes 262144 | tf_op jit(solution)/shard_map/psum | solution.py:84
Sparse Core Ops, SparseCore 0:
  208.1 39.2 reduce-scatter.3
Sparse Core Ops, SparseCore 1:
  211.7 242.6 all-reduce.1
